TPU v7x, 32 devices: a whole 2x2x4 slice. The times are simulated.
32 devices in a mesh: dp: 8 (over z, x), tensor: 4 (over y, core).
Axes of the slice: x: 2, y: 2, z: 4, core: 2. Of those that a mesh axis runs over, the one named last changes fastest.
Arguments:
- tokens: bfloat16 [32768, 768], P(('dp', 'tensor')), may hold values from -6 to 6
- cotangent: bfloat16 [32768, 768], P(('dp', 'tensor')), may hold values from -26 to 26
- seq_group: int32 [16], P('dp'), may hold values from 0 to 1
- block_slot: int32 [13830], replicated, may hold values from 0 to 20751, as said below
- master: float32 [4, 20752, 128], P('tensor', 'dp'), may hold values from -3 to 3
- first_moment: float32 [4, 20752, 128], P('tensor', 'dp'), may hold values from -1 to 1
- second_moment: float32 [4, 20752, 128], P('tensor', 'dp'), may hold values from 0 to 1, as said below
Outputs:
- output: bfloat16 [32768, 768], P(('dp', 'tensor'))
- input_grad: float32 [32768, 768], P(('dp', 'tensor'))
- group_norms: float32 [16], P('dp')
- new_master: float32 [4, 20752, 128], P('tensor', 'dp')
- new_first: float32 [4, 20752, 128], P('tensor', 'dp')
- new_second: float32 [4, 20752, 128], P('tensor', 'dp')
Inputs may be any that keep to these rules, and one draw needn't show every extreme that they name: `block_slot`: all entries differ; slot s belongs to the owner with dp index s // 2594; one owner holds 2594 blocks. `seq_group`: group ids count within one dp index: sequences of different dp indices never share a group. `second_moment`: Positive.
All inputs are finite; a program needn't handle non-finite values.
Results may differ from a plain program's by a relative error of at most 0.012.
Values may be sent and summed in bfloat16 or wider, within the bound.
No kernel may reach another device: no remote copies, remote signals or barrier semaphores. Data moves between devices by JAX's collectives and lax.ppermute only.
A program may use at most 256 MiB of HBM per device.

v0:
```python
import jax
import jax.numpy as jnp
from jax import lax
from jax.sharding import PartitionSpec as P

HEADS = 12
HD = 64
ROT = 16
FF = 3072
eps_norm = 1e-05
eps_adam = 1e-08
beta_one = 0.5
beta_two = 0.6
root_half = 0.7071067811865476
inv_root_tau = 0.3989422804014327


def rotary_tables(length, rot_dims):
    half_rot = rot_dims // 2
    frequency = 10000.0 ** (-2.0 * jnp.arange(half_rot, dtype=jnp.float32) / rot_dims)
    angles = jnp.arange(length, dtype=jnp.float32)[:, None] * frequency[None, :]
    return (jnp.cos(angles), jnp.sin(angles))


def rotate(features, cosine, sine_table, rot_dims):
    half_rot = rot_dims // 2
    first_half = features[..., :half_rot]
    second_half = features[..., half_rot:rot_dims]
    cos_cols = cosine[:, None, :]
    sin_cols = sine_table[:, None, :]
    return jnp.concatenate(
        [
            first_half * cos_cols - second_half * sin_cols,
            second_half * cos_cols + first_half * sin_cols,
            features[..., rot_dims:],
        ],
        axis=-1,
    )


def unrotate(grad_in, cosine, sine_table, rot_dims):
    half_rot = rot_dims // 2
    first_half = grad_in[..., :half_rot]
    second_half = grad_in[..., half_rot:rot_dims]
    cos_cols = cosine[:, None, :]
    sin_cols = sine_table[:, None, :]
    return jnp.concatenate(
        [
            first_half * cos_cols + second_half * sin_cols,
            second_half * cos_cols - first_half * sin_cols,
            grad_in[..., rot_dims:],
        ],
        axis=-1,
    )


def layer_norm(rows_in):
    row_mean = jnp.mean(rows_in, axis=-1, keepdims=True)
    centred = rows_in - row_mean
    inverse = lax.rsqrt(jnp.mean(centred * centred, axis=-1, keepdims=True) + eps_norm)
    return (centred * inverse, inverse)


def unpack(flat_params, d_model, heads_local, ff_local, width_local):
    inner_width = heads_local * HD
    end_qkv = d_model * 3 * inner_width
    end_out = end_qkv + inner_width * d_model
    end_up = end_out + d_model * ff_local
    end_down = end_up + ff_local * d_model
    return (
        flat_params[:end_qkv].reshape(d_model, 3 * inner_width),
        flat_params[end_qkv:end_out].reshape(inner_width, d_model),
        flat_params[end_out:end_up].reshape(d_model, ff_local),
        flat_params[end_up:end_down].reshape(ff_local, d_model),
        flat_params[end_down:].reshape(4, width_local),
    )


def step_rates(position, d_model, heads_local, head_dim, ff_local, seq_len, ff_all):
    end_qkv = d_model * 3 * heads_local * head_dim
    end_out = end_qkv + heads_local * head_dim * d_model
    end_up = end_out + d_model * ff_local
    end_down = end_up + ff_local * d_model
    matrix_rate = d_model ** (-0.5)
    learn_rate = jnp.where(
        position < end_qkv,
        matrix_rate,
        jnp.where(
            position < end_out,
            (seq_len / (5.0 * d_model)) ** 0.5,
            jnp.where(
                position < end_up,
                matrix_rate,
                jnp.where(position < end_down, ff_all ** (-0.5), 0.1),
            ),
        ),
    )
    weight_decay = jnp.where(position < end_down, 0.1, 0.0)
    return (learn_rate.astype(jnp.float32), weight_decay.astype(jnp.float32))


def adam_update(weight, moment_one, moment_two, gradient, learn_rate, weight_decay):
    new_one = beta_one * moment_one + (1.0 - beta_one) * gradient
    new_two = beta_two * moment_two + (1.0 - beta_two) * gradient * gradient
    new_weight = weight - learn_rate * (
        new_one / (jnp.sqrt(new_two) + eps_adam) + weight_decay * weight
    )
    return (new_weight, new_one, new_two)


def by_sequence(tensor_in, seq_count):
    return tensor_in.reshape(seq_count, -1, tensor_in.shape[-1])


def seq_product(left, right, seq_count):
    return jnp.einsum(
        "sli,slj->sij",
        by_sequence(left, seq_count),
        by_sequence(right, seq_count),
        preferred_element_type=jnp.float32,
    )


def on_device(tokens, cotangent, seq_group, block_slot, master, first_moment, second_moment):
    tensor_count = lax.axis_size("tensor")
    tensor_rank = lax.axis_index("tensor")
    owner_index = lax.axis_index("dp")
    owner_count = lax.axis_size("dp")
    d_model = tokens.shape[1]
    local_rows = tokens.shape[0]
    width_local = d_model // tensor_count
    heads_local = HEADS // tensor_count
    inner_width = heads_local * HD
    ff_local = FF // tensor_count
    seq_count = seq_group.shape[0]
    tok_count = local_rows * tensor_count
    seq_len = tok_count // seq_count
    capacity = master.shape[1]
    block_width = master.shape[2]
    block_count = block_slot.shape[0]
    copies = lax.all_gather(master[0].astype(jnp.bfloat16), "dp", axis=0, tiled=True)
    flat_params = copies[block_slot].reshape(-1)
    w_qkv, w_out, w_up, w_down, norm_local = unpack(
        flat_params, d_model, heads_local, ff_local, width_local
    )
    x_full, norm_rows = (
        lax.all_gather(tokens, "tensor", axis=0, tiled=True),
        lax.all_gather(norm_local.reshape(1, 4 * width_local), "tensor", axis=0, tiled=True),
    )
    norm_full = jnp.transpose(norm_rows.reshape(tensor_count, 4, width_local), (1, 0, 2)).reshape(
        4, d_model
    )
    rows_full = x_full.astype(jnp.float32)
    normed, inverse = layer_norm(rows_full)
    norm_gains = norm_full.astype(jnp.float32)
    first_in = (normed * norm_gains[0] + norm_gains[1]).astype(jnp.bfloat16)
    second_in = (normed * norm_gains[2] + norm_gains[3]).astype(jnp.bfloat16)
    projected = jnp.dot(first_in, w_qkv, preferred_element_type=jnp.float32).reshape(
        seq_count, seq_len, 3, heads_local, HD
    )
    cosine, sine_table = rotary_tables(seq_len, ROT)
    queries = rotate(projected[:, :, 0], cosine, sine_table, ROT).astype(jnp.bfloat16)
    key_rows = rotate(projected[:, :, 1], cosine, sine_table, ROT).astype(jnp.bfloat16)
    values = projected[:, :, 2].astype(jnp.bfloat16)
    block_rows = min(512, seq_len)
    block_total = seq_len // block_rows
    scale_factor = HD ** (-0.5)
    starts = jnp.arange(block_total, dtype=jnp.int32) * block_rows
    key_index = jnp.arange(seq_len, dtype=jnp.int32)

    def scores_of(row_start):
        query_block = lax.dynamic_slice_in_dim(queries, row_start, block_rows, 1)
        scores = (
            jnp.einsum("sqhd,skhd->shqk", query_block, key_rows, preferred_element_type=jnp.float32)
            * scale_factor
        )
        allowed = (row_start + jnp.arange(block_rows, dtype=jnp.int32))[:, None] >= key_index[
            None, :
        ]
        return (jnp.where(allowed, scores, -1e30), query_block)

    def forward_block(row_start):
        scores = scores_of(row_start)[0]
        row_peak = jnp.max(scores, axis=-1, keepdims=True)
        exp_scores = jnp.exp(scores - row_peak)
        row_total = jnp.sum(exp_scores, axis=-1, keepdims=True)
        weights_low = (exp_scores / row_total).astype(jnp.bfloat16)
        mixed_heads = jnp.einsum(
            "shqk,skhd->sqhd", weights_low, values, preferred_element_type=jnp.float32
        )
        return (mixed_heads, row_peak + jnp.log(row_total))

    mixed_heads, log_sums = lax.map(forward_block, starts)
    attended = jnp.moveaxis(mixed_heads, 0, 1).reshape(tok_count, inner_width).astype(jnp.bfloat16)
    hidden_pre = jnp.dot(second_in, w_up, preferred_element_type=jnp.float32)
    hidden_low = jax.nn.gelu(hidden_pre, approximate=False).astype(jnp.bfloat16)
    branch = jnp.dot(attended, w_out, preferred_element_type=jnp.float32) + jnp.dot(
        hidden_low, w_down, preferred_element_type=jnp.float32
    )
    branch_sum = lax.psum_scatter(
        branch.astype(jnp.bfloat16), "tensor", scatter_dimension=0, tiled=True
    ).astype(jnp.float32)
    output = (tokens.astype(jnp.float32) + branch_sum).astype(jnp.bfloat16)
    back_full = lax.all_gather(cotangent, "tensor", axis=0, tiled=True)
    grad_down = seq_product(hidden_low, back_full, seq_count)
    grad_hidden = jnp.dot(back_full, w_down.T, preferred_element_type=jnp.float32)
    cumulative = 0.5 * (1.0 + lax.erf(hidden_pre * root_half))
    density = jnp.exp(-0.5 * hidden_pre * hidden_pre) * inv_root_tau
    grad_pre = (grad_hidden * (cumulative + hidden_pre * density)).astype(jnp.bfloat16)
    grad_up = seq_product(second_in, grad_pre, seq_count)
    second_back = jnp.dot(grad_pre, w_up.T, preferred_element_type=jnp.float32)
    grad_out = seq_product(attended, back_full, seq_count)
    grad_attended = jnp.dot(back_full, w_out.T, preferred_element_type=jnp.float32).astype(
        jnp.bfloat16
    )
    grad_blocks_in = jnp.moveaxis(
        grad_attended.reshape(seq_count, block_total, block_rows, heads_local, HD), 1, 0
    )

    def backward_block(carried, inputs):
        row_start, log_sum, grad_block = inputs
        scores, query_block = scores_of(row_start)
        probs = jnp.exp(scores - log_sum)
        grad_probs = jnp.einsum(
            "sqhd,skhd->shqk", grad_block, values, preferred_element_type=jnp.float32
        )
        row_dot = jnp.sum(probs * grad_probs, axis=-1, keepdims=True)
        grad_scores = (probs * (grad_probs - row_dot)).astype(jnp.bfloat16)
        grad_query = (
            jnp.einsum("shqk,skhd->sqhd", grad_scores, key_rows, preferred_element_type=jnp.float32)
            * scale_factor
        )
        grad_keys = (
            carried[0]
            + jnp.einsum(
                "shqk,sqhd->skhd", grad_scores, query_block, preferred_element_type=jnp.float32
            )
            * scale_factor
        )
        grad_values = carried[1] + jnp.einsum(
            "shqk,sqhd->skhd",
            probs.astype(jnp.bfloat16),
            grad_block,
            preferred_element_type=jnp.float32,
        )
        return ((grad_keys, grad_values), grad_query)

    zero_heads = jnp.zeros((seq_count, seq_len, heads_local, HD), jnp.float32)
    key_value_grads, grad_queries = lax.scan(
        backward_block, (zero_heads, zero_heads), (starts, log_sums, grad_blocks_in)
    )
    grad_queries = jnp.moveaxis(grad_queries, 0, 1).reshape(seq_count, seq_len, heads_local, HD)
    grad_qkv = (
        jnp.stack(
            [
                unrotate(grad_queries, cosine, sine_table, ROT),
                unrotate(key_value_grads[0], cosine, sine_table, ROT),
                key_value_grads[1],
            ],
            axis=2,
        )
        .reshape(tok_count, 3 * inner_width)
        .astype(jnp.bfloat16)
    )
    grad_qkv_w = seq_product(first_in, grad_qkv, seq_count)
    first_back = jnp.dot(grad_qkv, w_qkv.T, preferred_element_type=jnp.float32)
    row_start_local = tensor_rank * local_rows
    first_sum, second_sum = (
        lax.psum_scatter(
            first_back.astype(jnp.bfloat16), "tensor", scatter_dimension=0, tiled=True
        ).astype(jnp.float32),
        lax.psum_scatter(
            second_back.astype(jnp.bfloat16), "tensor", scatter_dimension=0, tiled=True
        ).astype(jnp.float32),
    )
    normed_rows = lax.dynamic_slice_in_dim(normed, row_start_local, local_rows, 0)
    inverse_rows = lax.dynamic_slice_in_dim(inverse, row_start_local, local_rows, 0)
    scaled_first = first_sum * norm_gains[0]
    scaled_second = second_sum * norm_gains[2]
    first_mean = jnp.mean(scaled_first, axis=1, keepdims=True)
    first_cross = jnp.mean(scaled_first * normed_rows, axis=1, keepdims=True)
    second_mean = jnp.mean(scaled_second, axis=1, keepdims=True)
    second_cross = jnp.mean(scaled_second * normed_rows, axis=1, keepdims=True)
    grad_input = (
        cotangent.astype(jnp.float32)
        + inverse_rows * (scaled_first - first_mean - normed_rows * first_cross)
        + inverse_rows * (scaled_second - second_mean - normed_rows * second_cross)
    )
    row_seq = (row_start_local + jnp.arange(local_rows, dtype=jnp.int32)) // seq_len
    row_member = (row_seq[None, :] == jnp.arange(seq_count, dtype=jnp.int32)[:, None]).astype(
        jnp.float32
    )
    partial_sums = jnp.stack(
        [
            jnp.dot(row_member, first_sum * normed_rows, precision=lax.Precision.HIGHEST),
            jnp.dot(row_member, first_sum, precision=lax.Precision.HIGHEST),
            jnp.dot(row_member, second_sum * normed_rows, precision=lax.Precision.HIGHEST),
            jnp.dot(row_member, second_sum, precision=lax.Precision.HIGHEST),
        ],
        axis=1,
    )
    norm_grads = lax.psum_scatter(partial_sums, "tensor", scatter_dimension=2, tiled=True)
    per_seq = jnp.concatenate(
        [
            grad_qkv_w.reshape(seq_count, -1),
            grad_out.reshape(seq_count, -1),
            grad_up.reshape(seq_count, -1),
            grad_down.reshape(seq_count, -1),
            norm_grads.reshape(seq_count, -1),
        ],
        axis=1,
    )
    member = (seq_group[None, :] == jnp.arange(seq_count, dtype=jnp.int32)[:, None]).astype(
        jnp.float32
    )
    group_grads = jnp.dot(member, per_seq, precision=lax.Precision.HIGHEST)
    squares = lax.psum(jnp.sum(group_grads * group_grads, axis=1), "tensor")
    group_norms = jnp.sqrt(squares)
    clip_scale = 1.0 / jnp.maximum(group_norms, 1.0)
    clipped = jnp.dot(clip_scale, group_grads, precision=lax.Precision.HIGHEST)
    grad_rows = clipped.reshape(block_count, block_width)
    slot_total = owner_count * capacity
    slot_block = (
        jnp.full((slot_total,), -1, jnp.int32)
        .at[block_slot]
        .set(jnp.arange(block_count, dtype=jnp.int32))
    )
    my_blocks = lax.dynamic_slice_in_dim(slot_block, owner_index * capacity, capacity)
    summed = lax.psum(grad_rows, "dp")
    owned_grad = jnp.where(my_blocks[:, None] >= 0, summed[jnp.maximum(my_blocks, 0)], 0.0)
    position = (
        jnp.maximum(my_blocks, 0)[:, None] * block_width
        + jnp.arange(block_width, dtype=jnp.int32)[None, :]
    )
    learn_rate, weight_decay = step_rates(position, d_model, heads_local, HD, ff_local, seq_len, FF)
    new_weight, new_one, new_two = adam_update(
        master[0], first_moment[0], second_moment[0], owned_grad, learn_rate, weight_decay
    )
    return (output, grad_input, group_norms, new_weight[None], new_one[None], new_two[None])


def solution(mesh):
    placed = (
        P(("dp", "tensor"), None),
        P(("dp", "tensor"), None),
        P("dp"),
        P(),
        P("tensor", "dp", None),
        P("tensor", "dp", None),
        P("tensor", "dp", None),
    )
    return jax.shard_map(
        on_device,
        mesh=mesh,
        in_specs=placed,
        out_specs=(
            P(("dp", "tensor"), None),
            P(("dp", "tensor"), None),
            P("dp"),
            P("tensor", "dp", None),
            P("tensor", "dp", None),
            P("tensor", "dp", None),
        ),
        check_vma=False,
    )
```

profile of v0, /device:TPU:0, one launch (start us, length us, event | category | flops | bytes accessed | tf_op | source)
XLA Modules:
  0.0 1451.3 jit_solution(10674566761597092681)
XLA Ops:
  17.1 148.8 %all-gather.10.cloned.1.call-done = bf16[1,20752,128]{2,0,1:T(2,128)(2,1)} async-done(((bf16[1,2594,128]{2,0,1:T(2,128)(2,1)}), bf16[1,20752,128]{2,0,1:T(2,128)(2,1)}) %all-gather.10.cloned.1.call-update) | async-done | bytes 5312528 | tf_op jit(solution)/shard_map/all_gather | solution.py:141
  165.9 8.5 copy.115
  174.4 30.7 %gather_fusion = bf16[13830,128]{1,0:T(8,128)(2,1)S(1)} fusion(bf16[20752,128]{1,0:T(8,128)(2,1)} %bitcast.203, s32[14336]{0:T(1024)} %pad_clamp_fusion), kind=kCustom, calls=%fused_computation | custom fusion | bytes 7136280 | tf_op jit(solution)/shard_map/gather | solution.py:142
  234.9 7.9 fusion.36
  250.1 10.0 all-gather.8.cloned.1.call-done
  260.0 6.1 fusion.55
  276.1 163.2 %while.30 = (s32[]{:T(128)}, bf16[4,2,512,3,64]{2,4,3,1,0:T(8,128)(2,1)}, f32[4,2,3,512,1]{3,2,1,4,0:T(4,128)S(1)}, s32[4]{0:T(128)S(1)}, bf16[2,2048,3,64]{1,3,...) while((s32[]{:T(128)}, ...), condition=%wide.region_5.6_spmd.clone.clone, body=%wide.region_2.5_spmd.clone.sunk.clone | while | flops 1687156224 | bytes 96723152 | solution.py:193
  280.0 12.1 fusion.178
  292.1 12.1 fusion.179
  304.2 11.6 fusion.180
  320.8 12.1 fusion.178
  332.9 12.1 fusion.179
  345.0 11.6 fusion.180
  361.6 12.1 fusion.178
  373.7 12.1 fusion.179
  385.8 11.6 fusion.180
  402.4 12.1 fusion.178
  414.5 12.1 fusion.179
  426.6 11.6 fusion.180
  439.3 336.2 %while.31 = (s32[]{:T(128)}, f32[2,2048,3,64]{1,3,2,0:T(8,128)}, f32[2,2048,3,64]{1,3,2,0:T(8,128)}, f32[4,2,512,3,64]{2,4,3,1,0:T(8,128)}, s32[4]{0:T(128)S(1)}...) while((s32[]{:T(128)}, f32[2,2048,3,64]{1,3,2,0:T(8,128)}, ...), condition=%wide.region_9.10_spmd.clone.clone, body=%wide.region_7.9_spmd.clone.sunk.clone | while | flops 4126078464 | bytes 275603712 | solution.py:249
  443.5 11.3 fusion.190
  454.8 12.9 bitcast_add_fusion.7
  467.7 18.1 %multiply_reduce_fusion.4 = (f32[2,3,512]{2,1,0:T(4,128)S(1)}, f32[2,3,512,2048]{3,2,1,0:T(8,128)}) fusion(f32[2,3,512,2048]{3,2,1,0:T(8,128)} %fusion.190, f32[2,3,512]{2,1,0:T(4,128)S(1)} %dynamic-slice_bitcast_fusion.3, pred[512,2048]{1,0:T(8,128)(4,1)S(1)} %iota_compare_fusion.12, bf16[2,2048,3,64]{1,3,2,0:T(8,128)(2,1)} %copy-done.1, ...), kind=kOutput, calls=%fused_computation.22.clone.1.clone | convolution fusion | flops 836760576 | bytes 53370884 | tf_op jit(solution)/shard_map/while/body/eval_jaxpr/sqhd,skhd->shqk/dot_general | solution.py:224
  485.8 17.0 %multiply_convert_fusion.3 = bf16[2,3,512,2048]{3,2,1,0:T(8,128)(2,1)S(1)} fusion(f32[2,3,512,2048]{3,2,1,0:T(8,128)} %get-tuple-element.409, f32[2,3,512,2048]{3,2,1,0:T(8,128)} %fusion.190, f32[2,3,512]{2,1,0:T(4,128)S(1)} %get-tuple-element.410, f32[2,3,512]{2,1,0:T(4,128)S(1)} %dynamic-slice_bitcast_fusion.3, ...), kind=kLoop, calls=%fused_computation.21.clone.1.clone | loop fusion | flops 37748736 | bytes 63987712 | tf_op jit(solution)/shard_map/while/body/eval_jaxpr/convert_element_type | solution.py:228
  512.5 9.5 fusion.191
  526.0 11.3 fusion.190
  537.3 13.8 bitcast_add_fusion.7
  551.1 18.1 %multiply_reduce_fusion.4 = (f32[2,3,512]{2,1,0:T(4,128)S(1)}, f32[2,3,512,2048]{3,2,1,0:T(8,128)}) fusion(f32[2,3,512,2048]{3,2,1,0:T(8,128)} %fusion.190, f32[2,3,512]{2,1,0:T(4,128)S(1)} %dynamic-slice_bitcast_fusion.3, pred[512,2048]{1,0:T(8,128)(4,1)S(1)} %iota_compare_fusion.12, bf16[2,2048,3,64]{1,3,2,0:T(8,128)(2,1)} %copy-done.1, ...), kind=kOutput, calls=%fused_computation.22.clone.1.clone | convolution fusion | flops 836760576 | bytes 53370884 | tf_op jit(solution)/shard_map/while/body/eval_jaxpr/sqhd,skhd->shqk/dot_general | solution.py:224
  569.2 17.0 %multiply_convert_fusion.3 = bf16[2,3,512,2048]{3,2,1,0:T(8,128)(2,1)S(1)} fusion(f32[2,3,512,2048]{3,2,1,0:T(8,128)} %get-tuple-element.409, f32[2,3,512,2048]{3,2,1,0:T(8,128)} %fusion.190, f32[2,3,512]{2,1,0:T(4,128)S(1)} %get-tuple-element.410, f32[2,3,512]{2,1,0:T(4,128)S(1)} %dynamic-slice_bitcast_fusion.3, ...), kind=kLoop, calls=%fused_computation.21.clone.1.clone | loop fusion | flops 37748736 | bytes 63987712 | tf_op jit(solution)/shard_map/while/body/eval_jaxpr/convert_element_type | solution.py:228
  590.8 6.1 bitcast_add_fusion.6
  596.9 9.5 fusion.191
  610.4 11.3 fusion.190
  621.7 13.8 bitcast_add_fusion.7
  635.5 18.1 %multiply_reduce_fusion.4 = (f32[2,3,512]{2,1,0:T(4,128)S(1)}, f32[2,3,512,2048]{3,2,1,0:T(8,128)}) fusion(f32[2,3,512,2048]{3,2,1,0:T(8,128)} %fusion.190, f32[2,3,512]{2,1,0:T(4,128)S(1)} %dynamic-slice_bitcast_fusion.3, pred[512,2048]{1,0:T(8,128)(4,1)S(1)} %iota_compare_fusion.12, bf16[2,2048,3,64]{1,3,2,0:T(8,128)(2,1)} %copy-done.1, ...), kind=kOutput, calls=%fused_computation.22.clone.1.clone | convolution fusion | flops 836760576 | bytes 53370884 | tf_op jit(solution)/shard_map/while/body/eval_jaxpr/sqhd,skhd->shqk/dot_general | solution.py:224
  653.6 17.0 %multiply_convert_fusion.3 = bf16[2,3,512,2048]{3,2,1,0:T(8,128)(2,1)S(1)} fusion(f32[2,3,512,2048]{3,2,1,0:T(8,128)} %get-tuple-element.409, f32[2,3,512,2048]{3,2,1,0:T(8,128)} %fusion.190, f32[2,3,512]{2,1,0:T(4,128)S(1)} %get-tuple-element.410, f32[2,3,512]{2,1,0:T(4,128)S(1)} %dynamic-slice_bitcast_fusion.3, ...), kind=kLoop, calls=%fused_computation.21.clone.1.clone | loop fusion | flops 37748736 | bytes 63987712 | tf_op jit(solution)/shard_map/while/body/eval_jaxpr/convert_element_type | solution.py:228
  675.2 6.1 bitcast_add_fusion.6
  681.3 9.5 fusion.191
  694.8 11.3 fusion.190
  706.1 13.8 bitcast_add_fusion.7
  719.9 18.1 %multiply_reduce_fusion.4 = (f32[2,3,512]{2,1,0:T(4,128)S(1)}, f32[2,3,512,2048]{3,2,1,0:T(8,128)}) fusion(f32[2,3,512,2048]{3,2,1,0:T(8,128)} %fusion.190, f32[2,3,512]{2,1,0:T(4,128)S(1)} %dynamic-slice_bitcast_fusion.3, pred[512,2048]{1,0:T(8,128)(4,1)S(1)} %iota_compare_fusion.12, bf16[2,2048,3,64]{1,3,2,0:T(8,128)(2,1)} %copy-done.1, ...), kind=kOutput, calls=%fused_computation.22.clone.1.clone | convolution fusion | flops 836760576 | bytes 53370884 | tf_op jit(solution)/shard_map/while/body/eval_jaxpr/sqhd,skhd->shqk/dot_general | solution.py:224
  738.0 17.0 %multiply_convert_fusion.3 = bf16[2,3,512,2048]{3,2,1,0:T(8,128)(2,1)S(1)} fusion(f32[2,3,512,2048]{3,2,1,0:T(8,128)} %get-tuple-element.409, f32[2,3,512,2048]{3,2,1,0:T(8,128)} %fusion.190, f32[2,3,512]{2,1,0:T(4,128)S(1)} %get-tuple-element.410, f32[2,3,512]{2,1,0:T(4,128)S(1)} %dynamic-slice_bitcast_fusion.3, ...), kind=kLoop, calls=%fused_computation.21.clone.1.clone | loop fusion | flops 37748736 | bytes 63987712 | tf_op jit(solution)/shard_map/while/body/eval_jaxpr/convert_element_type | solution.py:228
  765.7 9.5 fusion.191
  788.4 9.5 copy.74
  813.7 9.7 fusion.108
  828.9 9.4 convolution_convert_fusion
  840.7 33.3 %fusion.41 = (bf16[4096,768]{1,0:T(8,128)(2,1)}, f32[4096,768]{1,0:T(8,128)S(1)}) fusion(bf16[4096,768]{1,0:T(8,128)(2,1)} %get-tuple-element.243, bf16[768,768]{1,0:T(8,128)(2,1)S(1)} %copy-done.22), kind=kOutput, calls=%fused_computation.59 | convolution fusion | flops 5036310528 | bytes 26345472 | tf_op jit(solution)/shard_map/dot_general | solution.py:195
  874.0 9.2 fusion.47
  885.8 7.0 convolution_convert_fusion.1
  892.8 9.4 convolution_bitcast_fusion.1
  909.1 6.2 constant_dynamic-update-slice_fusion.2
  917.7 12.2 convolution_bitcast_fusion
  929.9 11.5 fusion.107
  946.8 21.3 %reduce-scatter.11.cloned.1.call-done = bf16[1024,768]{1,0:T(8,128)(2,1)} async-done(((bf16[4096,768]{1,0:T(8,128)(2,1)}), bf16[1024,768]{1,0:T(8,128)(2,1)}) %reduce-scatter.11.cloned.1.call-update) | async-done | bytes 1572880 | tf_op jit(solution)/shard_map/reduce_scatter | solution.py:272
  977.0 9.1 add_convert_fusion
  986.1 8.1 copy.103
  1002.3 41.5 %multiply_reduce_fusion.1 = (f32[2]{0:T(128)S(1)}, f32[2,1770240]{1,0:T(2,128)}) fusion(f32[2,1770240]{1,0:T(2,128)} %constant_dynamic-update-slice_fusion, s32[2]{0:T(128)S(1)} %copy-done.37), kind=kOutput, calls=%fused_computation.55 | convolution fusion | flops 92052480 | bytes 28323856 | tf_op jit(solution)/shard_map/dot_general | solution.py:316
  1043.8 6.4 psum.14
  1050.1 119.3 %convolution_reduce_fusion = f32[1770240]{0:T(1024)} fusion(f32[2,1770240]{1,0:T(2,128)} %get-tuple-element.263, f32[2]{0:T(128)S(1)} %sqrt.7), kind=kOutput, calls=%fused_computation.116 | convolution fusion | flops 42485764 | bytes 21242888 | tf_op jit(solution)/shard_map/dot_general | solution.py:320
  1169.4 65.6 %scatter_custom_fusion = s32[20752]{0:T(1024)S(1)} fusion(s32[13830]{0:T(1024)} %copy-done.27, s32[13830]{0:T(1024)S(1)} %iota.92, s32[]{:T(128)} %constant.72.clone.1), kind=kCustom, calls=%fused_computation.158 | custom fusion | bytes 83520 | tf_op jit(solution)/shard_map/scatter | solution.py:326
  1246.7 157.5 %all-reduce.2.cloned.1.call-done = f32[13830,128]{1,0:T(8,128)} async-done(((f32[13830,128]{1,0:T(8,128)}), f32[13830,128]{1,0:T(8,128)}) %all-reduce.2.cloned.1.call-update) | async-done | bytes 7080976 | tf_op jit(solution)/shard_map/psum | solution.py:329
  1404.2 7.7 gather_fusion.1
  1417.1 9.0 copy.86
  1426.1 9.0 copy.88
  1435.1 9.0 copy.87
  (270 shorter events, 193.2 us)
Async XLA Ops:
  7.2 7.7 copy-start.35
  7.2 158.7 %all-gather.10.cloned.1.call-start = ((), (), s32[]{:S(2)}) async-start(), calls=%async_computation.10 | async-start | bytes 11953152 | tf_op jit(solution)/shard_map/all_gather | solution.py:141
  10.8 217.5 %all-gather.6.cloned.1.call-start = ((), (), s32[]{:S(2)}) async-start(), calls=%async_computation.4 | async-start | bytes 7864320 | tf_op jit(solution)/shard_map/all_gather | solution.py:147
  11.6 248.4 %all-gather.8.cloned.1.call-start = ((), (), s32[]{:S(2)}) async-start(), calls=%async_computation.6 | async-start | bytes 7864320 | tf_op jit(solution)/shard_map/all_gather | solution.py:204
  12.3 929.1 %reduce-scatter.9.cloned.1.call-start = ((), (), s32[]{:S(2)}) async-start(), calls=%async_computation.7 | async-start | bytes 7864320 | tf_op jit(solution)/shard_map/reduce_scatter | solution.py:269
  214.3 20.6 %copy-start.31 = (f32[768]{0:T(1024)}, f32[768]{0:T(1024)S(1)}, u32[]{:S(2)}) copy-start(f32[768]{0:T(1024)S(1)} %mul.459) | copy-start | bytes 9220
  214.4 20.5 %copy-start.33 = (f32[768]{0:T(1024)}, f32[768]{0:T(1024)S(1)}, u32[]{:S(2)}) copy-start(f32[768]{0:T(1024)S(1)} %mul.475) | copy-start | bytes 9220
  220.0 6.4 copy-start.16
  225.8 6.4 copy-start.17
  228.3 4.7 copy-start.3
  232.2 2.7 copy-start.36
  234.9 7.9 copy-start.30
  242.8 3.9 copy-start.12
  246.9 13.1 copy-start.18
  269.5 3.6 copy-start.11
  269.5 3.8 copy-start.23
  269.5 3.8 copy-start.25
  273.3 2.8 copy-start.29
  273.3 2.8 copy-start.39
  292.1 12.1 copy-start.7
  332.9 12.1 copy-start.7
  373.7 12.1 copy-start.7
  414.5 12.1 copy-start.7
  439.5 3.3 copy-start.1
  502.9 4.5 copy-start
  512.5 9.5 copy-start.2
  522.0 3.3 copy-start.1
  586.3 4.5 copy-start
  596.9 9.5 copy-start.2
  606.4 3.3 copy-start.1
  670.7 4.5 copy-start
  681.3 9.5 copy-start.2
  690.9 3.3 copy-start.1
  755.1 4.5 copy-start
  765.7 9.5 copy-start.2
  775.6 4.1 copy-start.24
  775.6 4.1 copy-start.26
  788.4 9.5 copy-start.9
  799.1 9.3 slice-start
  801.7 6.7 slice-start.1
  806.5 7.2 slice-start.4
  808.4 5.2 slice-start.5
  838.3 129.8 %reduce-scatter.11.cloned.1.call-start = ((), (), s32[]{:S(2)}) async-start(), calls=%async_computation.8 | async-start | bytes 7864320 | tf_op jit(solution)/shard_map/reduce_scatter | solution.py:272
  838.3 35.7 %slice-start.2 = ((s8[6291456]{0:T(1024)(128)(4,1)}), s8[4194304]{0:T(1024)(128)(4,1)S(1)}, s32[]{:S(2)}) async-start(s8[6291456]{0:T(1024)(128)(4,1)} %bitcast.218), calls=%async_computation.14 | async-start | bytes 8388608
  840.6 33.3 %slice-start.3 = ((s8[6291456]{0:T(1024)(128)(4,1)}), s8[2097152]{0:T(1024)(128)(4,1)S(1)}, s32[]{:S(2)}) async-start(s8[6291456]{0:T(1024)(128)(4,1)} %bitcast.218), calls=%async_computation.15 | async-start | bytes 4194304
  840.7 33.3 %copy-start.20 = (bf16[768,768]{1,0:T(8,128)(2,1)S(1)}, bf16[768,768]{1,0:T(8,128)(2,1)}, u32[]{:S(2)}) copy-start(bf16[768,768]{1,0:T(8,128)(2,1)} %reshape.377) | copy-start | bytes 3538948
  883.2 2.6 copy-start.38
  902.2 5.8 copy-start.15
  909.1 91.2 %reduce-scatter.13.cloned.1.call-start = ((), (), s32[]{:S(2)}) async-start(), calls=%async_computation.11 | async-start | bytes 491520
  909.1 6.2 copy-start.10
  917.7 12.2 copy-start.21
  929.9 11.5 copy-start.28
  946.8 30.2 %copy-start.19 = (bf16[192,768]{1,0:T(8,128)(2,1)S(1)}, bf16[192,768]{1,0:T(8,128)(2,1)}, u32[]{:S(2)}) copy-start(bf16[192,768]{1,0:T(8,128)(2,1)} %reshape.375) | copy-start | bytes 884740
  968.1 3.8 copy-start.6
  976.5 262.1 %reduce-scatter.7.cloned.1.call-start = ((), (), s32[]{:S(2)}) async-start(), calls=%async_computation.5 | async-start | bytes 7864320 | tf_op jit(solution)/shard_map/reduce_scatter | solution.py:200
  994.2 410.0 %all-reduce.2.cloned.1.call-start = ((), (), s32[]{:S(2)}) async-start(), calls=%async_computation.9 | async-start | bytes 14163968 | tf_op jit(solution)/shard_map/psum | solution.py:329
  994.3 8.0 copy-start.37
  1050.1 119.3 %copy-start.40 = (f32[2]{0:T(128)}, f32[2]{0:T(128)S(1)}, u32[]{:S(2)}) copy-start(f32[2]{0:T(128)S(1)} %sqrt.7) | copy-start | bytes 28
  1169.4 65.9 %copy-start.5 = (bf16[1024,768]{1,0:T(8,128)(2,1)S(1)}, bf16[1024,768]{1,0:T(8,128)(2,1)}, u32[]{:S(2)}) copy-start(bf16[1024,768]{1,0:T(8,128)(2,1)} %reduce-scatter.9.cloned.1.call-done) | copy-start | bytes 4718596
  1169.4 65.9 %copy-start.32 = (f32[768]{0:T(1024)S(1)}, f32[768]{0:T(1024)}, u32[]{:S(2)}) copy-start(f32[768]{0:T(1024)} %copy-done.31) | copy-start | bytes 9220
  1169.4 65.9 %copy-start.34 = (f32[768]{0:T(1024)S(1)}, f32[768]{0:T(1024)}, u32[]{:S(2)}) copy-start(f32[768]{0:T(1024)} %copy-done.33) | copy-start | bytes 9220
  1235.3 7.0 dynamic-slice-start
  1238.6 3.6 copy-start.13
  1246.7 165.3 %copy-start.14 = (f32[1,2594,128]{2,0,1:T(1,128)S(1)}, f32[1,2594,128]{2,0,1:T(1,128)}, u32[]{:S(2)}) copy-start(f32[1,2594,128]{2,0,1:T(1,128)} %param.15) | copy-start | bytes 3984388
  (7 other events, 9.8 us)
Sparse Core Ops, SparseCore 0:
  10.9 154.8 all-gather.9
  167.4 44.5 all-gather.5
  213.6 46.4 all-gather.7
  838.4 58.8 reduce-scatter.8
  909.2 58.8 reduce-scatter.10
  976.7 20.7 reduce-scatter.12
  1000.0 58.9 reduce-scatter.6
  1169.5 234.6 all-reduce.1
where the time goes:
time: 1460 us; the launch traced here: 1450 us
  matrix products  624 us (43%)
  waiting for transfers between devices  339 us (23%)
  local copies, waits for them, and re-layouts  273 us (19%)
  other arithmetic  172 us (12%)
  loops' own time  16.5 us (1%)
  between operations  15.2 us (1%)
    psum x1, waiting for transfers between devices, on_device(): summed = lax.psum(grad_rows, 'dp')  158 us
    all_gather x1, waiting for transfers between devices, on_device(): lax.all_gather(master[0].astype(jnp.bfloat16), 'dp', axis=0, tiled=True)  149 us
    dot_general x1, matrix products, on_device(): clipped = jnp.dot(clip_scale, group_grads, precision=lax.Precision.HIGHEST)  119 us
    dot_general x8, matrix products, scores_of(): jnp.einsum('sqhd,skhd->shqk', query_block, key_rows, preferred_element_ty...  93.7 us
    unnamed x100, local copies, waits for them, and re-layouts  83.8 us
    dot_general x4, matrix products, backward_block(): jnp.einsum('sqhd,skhd->shqk', grad_block, values, preferred_element_type=...  72.5 us
    convert_element_type x4, other arithmetic, backward_block(): grad_scores = (probs * (grad_probs - row_dot)).astype(jnp.bfloat16)  68.2 us
    scatter x1, local copies, waits for them, and re-layouts, on_device(): slot_block = jnp.full((slot_total,), -1, jnp.int32).at[block_slot].set(jn...  65.6 us
  transfers between devices with their start and end apart: 8, of which 4 were waited for; matrix products, arithmetic and copies ran while one was open for 31% of the time, Pallas kernels for 0%

commit v1 on v0

--- a/solution.py
+++ b/solution.py
@@ -326,7 +326,11 @@
         .set(jnp.arange(block_count, dtype=jnp.int32))
     )
     my_blocks = lax.dynamic_slice_in_dim(slot_block, owner_index * capacity, capacity)
-    summed = lax.psum(grad_rows, "dp")
+    size = lax.axis_size("dp")
+    summed, far = (grad_rows, 1)
+    while far < size:
+        summed = summed + lax.ppermute(summed, "dp", [(i, i ^ far) for i in range(size)])
+        far = 2 * far
     owned_grad = jnp.where(my_blocks[:, None] >= 0, summed[jnp.maximum(my_blocks, 0)], 0.0)
     position = (
         jnp.maximum(my_blocks, 0)[:, None] * block_width

time: 1460 us -> 1840 us (1.26)
  waiting for transfers between devices: 339 us -> 721 us
  matrix products: 624 us -> 597 us
  other arithmetic: 172 us -> 194 us
    ppermute x0 -> x3, waiting for transfers between devices: none -> 513 us  [on_device(): lax.ppermute(summed, 'dp', [(i, i ^ far) for i in range(size)])]
    psum x1 -> x0, waiting for transfers between devices: 158 us -> none  [on_device(): summed = lax.psum(grad_rows, 'dp')]
    add x0 -> x3, other arithmetic: none -> 22.8 us  [on_device(): summed + lax.ppermute(summed, 'dp', [(i, i ^ far) for i in range(size)])]
    unnamed x100 -> x106, local copies, waits for them, and re-layouts: 83.8 us -> 81.6 us
  transfers between devices with their start and end apart: 8 -> 10, of which waited for: 4 -> 7; matrix products, arithmetic and copies ran while one was open for 31% -> 16% of each run, Pallas kernels for 0% -> 0%
where the time goes in v1:
time: 1840 us; the launch traced here: 1830 us
  waiting for transfers between devices  721 us (39%)
  matrix products  597 us (32%)
  local copies, waits for them, and re-layouts  273 us (15%)
  other arithmetic  194 us (11%)
    ppermute x3, waiting for transfers between devices, on_device(): lax.ppermute(summed, 'dp', [(i, i ^ far) for i in range(size)])  513 us
    all_gather x1, waiting for transfers between devices, on_device(): lax.all_gather(master[0].astype(jnp.bfloat16), 'dp', axis=0, tiled=True)  149 us
    dot_general x1, matrix products, on_device(): clipped = jnp.dot(clip_scale, group_grads, precision=lax.Precision.HIGHEST)  104 us
    dot_general x8, matrix products, scores_of(): jnp.einsum('sqhd,skhd->shqk', query_block, key_rows, preferred_element_ty...  93.8 us
    unnamed x106, local copies, waits for them, and re-layouts  81.6 us
    dot_general x4, matrix products, backward_block(): jnp.einsum('sqhd,skhd->shqk', grad_block, values, preferred_element_type=...  72.6 us
    convert_element_type x4, other arithmetic, backward_block(): grad_scores = (probs * (grad_probs - row_dot)).astype(jnp.bfloat16)  68.2 us
    scatter x1, local copies, waits for them, and re-layouts, on_device(): slot_block = jnp.full((slot_total,), -1, jnp.int32).at[block_slot].set(jn...  65.5 us
  transfers between devices with their start and end apart: 10, of which 7 were waited for; matrix products, arithmetic and copies ran while one was open for 16% of the time, Pallas kernels for 0%

profile of v1, /device:TPU:0, one launch (start us, length us, event | category | flops | bytes accessed | tf_op | source)
XLA Modules:
  0.0 1832.6 jit_solution(11544767130036350931)
XLA Ops:
  17.1 148.7 %all-gather.10.cloned.1.call-done = bf16[1,20752,128]{2,0,1:T(2,128)(2,1)} async-done(((bf16[1,2594,128]{2,0,1:T(2,128)(2,1)}), bf16[1,20752,128]{2,0,1:T(2,128)(2,1)}) %all-gather.10.cloned.1.call-update) | async-done | bytes 5312528 | tf_op jit(solution)/shard_map/all_gather | solution.py:141
  165.9 8.5 copy.115
  174.4 30.7 %gather_fusion = bf16[13830,128]{1,0:T(8,128)(2,1)S(1)} fusion(bf16[20752,128]{1,0:T(8,128)(2,1)} %bitcast.206, s32[14336]{0:T(1024)} %pad_clamp_fusion), kind=kCustom, calls=%fused_computation | custom fusion | bytes 7136280 | tf_op jit(solution)/shard_map/gather | solution.py:142
  234.8 7.9 fusion.36
  249.9 10.1 all-gather.8.cloned.1.call-done
  276.0 163.2 %while.30 = (s32[]{:T(128)}, bf16[4,2,512,3,64]{2,4,3,1,0:T(8,128)(2,1)}, f32[4,2,3,512,1]{3,2,1,4,0:T(4,128)S(1)}, s32[4]{0:T(128)S(1)}, bf16[2,2048,3,64]{1,3,...) while((s32[]{:T(128)}, ...), condition=%wide.region_5.6_spmd.clone.clone, body=%wide.region_2.5_spmd.clone.sunk.clone | while | flops 1687156224 | bytes 96723152 | solution.py:193
  279.9 12.1 fusion.179
  292.0 12.1 fusion.180
  304.1 11.6 fusion.181
  320.7 12.1 fusion.179
  332.8 12.1 fusion.180
  344.9 11.6 fusion.181
  361.5 12.1 fusion.179
  373.6 12.1 fusion.180
  385.7 11.6 fusion.181
  402.3 12.1 fusion.179
  414.4 12.1 fusion.180
  426.5 11.6 fusion.181
  439.2 336.3 %while.31 = (s32[]{:T(128)}, f32[2,2048,3,64]{1,3,2,0:T(8,128)}, f32[2,2048,3,64]{1,3,2,0:T(8,128)}, f32[4,2,512,3,64]{2,4,3,1,0:T(8,128)}, s32[4]{0:T(128)S(1)}...) while((s32[]{:T(128)}, f32[2,2048,3,64]{1,3,2,0:T(8,128)}, ...), condition=%wide.region_9.10_spmd.clone.clone, body=%wide.region_7.9_spmd.clone.sunk.clone | while | flops 4126078464 | bytes 275603712 | solution.py:249
  443.4 11.3 fusion.191
  454.7 12.9 bitcast_add_fusion.8
  467.6 18.1 multiply_reduce_fusion.4
  485.8 17.0 multiply_convert_fusion.3
  512.4 9.5 fusion.192
  525.9 11.3 fusion.191
  537.2 13.8 bitcast_add_fusion.8
  551.0 18.1 multiply_reduce_fusion.4
  569.1 17.0 multiply_convert_fusion.3
  590.7 6.1 bitcast_add_fusion.7
  596.8 9.5 fusion.192
  610.3 11.3 fusion.191
  621.6 13.8 bitcast_add_fusion.8
  635.4 18.1 multiply_reduce_fusion.4
  653.6 17.0 multiply_convert_fusion.3
  681.2 9.5 fusion.192
  694.7 11.3 fusion.191
  706.0 13.8 bitcast_add_fusion.8
  719.8 18.1 multiply_reduce_fusion.4
  737.9 17.0 multiply_convert_fusion.3
  765.6 9.5 fusion.192
  788.3 9.6 copy.74
  813.6 9.8 fusion.108
  828.8 9.3 convolution_convert_fusion
  840.6 33.3 %fusion.41 = (bf16[4096,768]{1,0:T(8,128)(2,1)}, f32[4096,768]{1,0:T(8,128)S(1)}) fusion(bf16[4096,768]{1,0:T(8,128)(2,1)} %get-tuple-element.243, bf16[768,768]{1,0:T(8,128)(2,1)S(1)} %copy-done.23), kind=kOutput, calls=%fused_computation.59 | convolution fusion | flops 5036310528 | bytes 26345472 | tf_op jit(solution)/shard_map/dot_general | solution.py:195
  874.0 9.2 fusion.47
  885.7 7.1 convolution_convert_fusion.1
  892.9 9.2 convolution_bitcast_fusion.1
  909.0 7.3 constant_dynamic-update-slice_fusion.2
  916.2 8.0 convolution_bitcast_fusion
  935.8 32.1 %reduce-scatter.11.cloned.1.call-done = bf16[1024,768]{1,0:T(8,128)(2,1)} async-done(((bf16[4096,768]{1,0:T(8,128)(2,1)}), bf16[1024,768]{1,0:T(8,128)(2,1)}) %reduce-scatter.11.cloned.1.call-update) | async-done | bytes 1572880 | tf_op jit(solution)/shard_map/reduce_scatter | solution.py:272
  980.2 14.9 reduce-scatter.13.cloned.1.call-done
  997.1 41.5 %multiply_reduce_fusion.1 = (f32[2]{0:T(128)S(1)}, f32[2,1770240]{1,0:T(2,128)}) fusion(f32[2,1770240]{1,0:T(2,128)} %constant_dynamic-update-slice_fusion, s32[2]{0:T(128)S(1)} %copy-done.38), kind=kOutput, calls=%fused_computation.55 | convolution fusion | flops 92052480 | bytes 28323856 | tf_op jit(solution)/shard_map/dot_general | solution.py:316
  1044.4 103.7 %convolution_reduce_fusion = f32[1770240]{0:T(1024)S(1)} fusion(f32[2,1770240]{1,0:T(2,128)} %get-tuple-element.263, f32[2]{0:T(128)S(1)} %sqrt.7), kind=kOutput, calls=%fused_computation.116 | convolution fusion | flops 42485764 | bytes 21242888 | tf_op jit(solution)/shard_map/dot_general | solution.py:320
  1149.8 152.5 %collective-permute-done = f32[13830,128]{1,0:T(8,128)S(1)} collective-permute-done((f32[13830,128]{1,0:T(8,128)S(1)}, f32[13830,128]{1,0:T(8,128)S(1)}, u32[]{:S(2)}, u32[]{:S(2)}) %collective-permute-start) | collective-permute-done | bytes 7080992 | tf_op jit(solution)/shard_map/ppermute | solution.py:332
  1314.0 7.7 fusion.107
  1326.3 134.6 %collective-permute-done.1 = f32[13830,128]{1,0:T(8,128)} collective-permute-done((f32[13830,128]{1,0:T(8,128)}, f32[13830,128]{1,0:T(8,128)}, u32[]{:S(2)}, u32[]{:S(2)}) %collective-permute-start.1) | collective-permute-done | bytes 7080992 | tf_op jit(solution)/shard_map/ppermute | solution.py:332
  1460.9 10.7 fusion.144
  1473.8 65.5 %scatter_custom_fusion = s32[20752]{0:T(1024)S(1)} fusion(s32[13830]{0:T(1024)} %copy-done.28, s32[13830]{0:T(1024)S(1)} %iota.92, s32[]{:T(128)} %constant.72.clone.1), kind=kCustom, calls=%fused_computation.158 | custom fusion | bytes 83520 | tf_op jit(solution)/shard_map/scatter | solution.py:326
  1550.9 226.1 %collective-permute-done.2 = f32[13830,128]{1,0:T(8,128)} collective-permute-done((f32[13830,128]{1,0:T(8,128)}, f32[13830,128]{1,0:T(8,128)}, u32[]{:S(2)}, u32[]{:S(2)}) %collective-permute-start.2) | collective-permute-done | bytes 7080992 | tf_op jit(solution)/shard_map/ppermute | solution.py:332
  1777.0 8.5 add.239
  1785.5 7.8 gather_fusion.1
  1798.6 9.0 copy.86
  1807.6 9.0 copy.88
  1816.5 9.0 copy.87
  (283 shorter events, 232.2 us)
Async XLA Ops:
  7.2 7.7 copy-start.36
  7.2 158.7 %all-gather.10.cloned.1.call-start = ((), (), s32[]{:S(2)}) async-start(), calls=%async_computation.9 | async-start | bytes 11953152 | tf_op jit(solution)/shard_map/all_gather | solution.py:141
  10.8 217.4 %all-gather.6.cloned.1.call-start = ((), (), s32[]{:S(2)}) async-start(), calls=%async_computation.4 | async-start | bytes 7864320 | tf_op jit(solution)/shard_map/all_gather | solution.py:147
  11.6 248.4 %all-gather.8.cloned.1.call-start = ((), (), s32[]{:S(2)}) async-start(), calls=%async_computation.6 | async-start | bytes 7864320 | tf_op jit(solution)/shard_map/all_gather | solution.py:204
  12.3 917.7 %reduce-scatter.9.cloned.1.call-start = ((), (), s32[]{:S(2)}) async-start(), calls=%async_computation.7 | async-start | bytes 7864320 | tf_op jit(solution)/shard_map/reduce_scatter | solution.py:269
  214.3 20.5 %copy-start.32 = (f32[768]{0:T(1024)}, f32[768]{0:T(1024)S(1)}, u32[]{:S(2)}) copy-start(f32[768]{0:T(1024)S(1)} %mul.459) | copy-start | bytes 9220
  214.4 20.4 %copy-start.34 = (f32[768]{0:T(1024)}, f32[768]{0:T(1024)S(1)}, u32[]{:S(2)}) copy-start(f32[768]{0:T(1024)S(1)} %mul.475) | copy-start | bytes 9220
  220.0 6.4 copy-start.18
  225.7 6.4 copy-start.19
  228.2 4.7 copy-start.3
  234.8 7.9 copy-start.31
  242.7 3.9 copy-start.14
  246.8 13.2 copy-start.20
  269.4 3.6 copy-start.13
  269.5 3.8 copy-start.24
  269.5 3.8 copy-start.26
  292.0 12.1 copy-start.9
  332.8 12.1 copy-start.9
  373.6 12.1 copy-start.9
  414.4 12.1 copy-start.9
  439.4 3.3 copy-start.1
  502.8 4.5 copy-start
  512.4 9.5 copy-start.2
  521.9 3.3 copy-start.1
  586.2 4.5 copy-start
  596.8 9.5 copy-start.2
  606.4 3.3 copy-start.1
  670.6 4.5 copy-start
  681.2 9.5 copy-start.2
  755.0 4.5 copy-start
  765.6 9.5 copy-start.2
  775.5 4.1 copy-start.25
  775.5 4.1 copy-start.27
  788.3 9.6 copy-start.11
  799.1 9.3 slice-start
  801.6 6.8 slice-start.1
  806.4 7.1 slice-start.6
  808.4 5.2 slice-start.7
  838.2 129.7 %reduce-scatter.11.cloned.1.call-start = ((), (), s32[]{:S(2)}) async-start(), calls=%async_computation.8 | async-start | bytes 7864320 | tf_op jit(solution)/shard_map/reduce_scatter | solution.py:272
  838.3 35.7 %slice-start.2 = ((s8[6291456]{0:T(1024)(128)(4,1)}), s8[4194304]{0:T(1024)(128)(4,1)S(1)}, s32[]{:S(2)}) async-start(s8[6291456]{0:T(1024)(128)(4,1)} %bitcast.220), calls=%async_computation.13 | async-start | bytes 8388608
  840.6 33.4 %slice-start.3 = ((s8[6291456]{0:T(1024)(128)(4,1)}), s8[2097152]{0:T(1024)(128)(4,1)S(1)}, s32[]{:S(2)}) async-start(s8[6291456]{0:T(1024)(128)(4,1)} %bitcast.220), calls=%async_computation.14 | async-start | bytes 4194304
  840.6 33.4 %copy-start.22 = (bf16[768,768]{1,0:T(8,128)(2,1)S(1)}, bf16[768,768]{1,0:T(8,128)(2,1)}, u32[]{:S(2)}) copy-start(bf16[768,768]{1,0:T(8,128)(2,1)} %reshape.377) | copy-start | bytes 3538948
  902.1 5.8 copy-start.17
  908.9 7.3 slice-start.4
  908.9 86.2 %reduce-scatter.13.cloned.1.call-start = ((), (), s32[]{:S(2)}) async-start(), calls=%async_computation.10 | async-start | bytes 491520
  909.0 7.3 slice-start.5
  924.2 5.8 copy-start.29
  967.9 3.8 copy-start.8
  974.2 568.6 %reduce-scatter.7.cloned.1.call-start = ((), (), s32[]{:S(2)}) async-start(), calls=%async_computation.5 | async-start | bytes 7864320 | tf_op jit(solution)/shard_map/reduce_scatter | solution.py:200
  974.2 22.9 %copy-start.38 = (s32[2]{0:T(128)S(1)}, s32[2]{0:T(128)}, u32[]{:S(2)}) copy-start(s32[2]{0:T(128)} %param.13) | copy-start | bytes 28
  1044.4 103.7 %copy-start.41 = (f32[2]{0:T(128)}, f32[2]{0:T(128)S(1)}, u32[]{:S(2)}) copy-start(f32[2]{0:T(128)S(1)} %sqrt.7) | copy-start | bytes 28
  1148.1 157.8 %copy-start.5 = (f32[1770240]{0:T(1024)}, f32[1770240]{0:T(1024)S(1)}, u32[]{:S(2)}) copy-start(f32[1770240]{0:T(1024)S(1)} %convolution_reduce_fusion) | copy-start | bytes 21242884
  1148.1 160.7 %copy-start.12 = (bf16[4,2,512,3,64]{2,4,3,1,0:T(8,128)(2,1)S(1)}, bf16[4,2,512,3,64]{2,4,3,1,0:T(8,128)(2,1)}, u32[]{:S(2)}) copy-start(bf16[4,2,512,3,64]{2,4,3,1,0:T(8,128)(2,1)} %get-tuple-element.108) | copy-start | bytes 4718596
  1148.1 154.2 %collective-permute-start = (f32[13830,128]{1,0:T(8,128)S(1)}, f32[13830,128]{1,0:T(8,128)S(1)}, u32[]{:S(2)}, u32[]{:S(2)}) collective-permute-start(f32[13830,128]{1,0:T(8,128)S(1)} %bitcast.207), channel_id=1, source_target_pairs={{0,4},{4,0},{8,12},{12,8},{16,20},{20,16},{24,28},{28,24},{1,5},{5... | collective-permute-start | bytes 21242888 | tf_op jit(solution)/shard_map/ppermute | solution.py:332
  1302.3 5.0 copy-start.6
  1307.3 153.6 %collective-permute-start.1 = (f32[13830,128]{1,0:T(8,128)}, f32[13830,128]{1,0:T(8,128)}, u32[]{:S(2)}, u32[]{:S(2)}) collective-permute-start(f32[13830,128]{1,0:T(8,128)} %bitcast_add_fusion.2), channel_id=1, source_target_pairs={{0,8},{4,12},{8,0},{12,4},{16,24},{20,28},{24,16},{28,20},{1,9},{5... | collective-permute-start | bytes 21242888 | tf_op jit(solution)/shard_map/ppermute | solution.py:332
  1314.0 7.7 copy-start.21
  1326.3 213.2 %copy-start.7 = (bf16[1024,768]{1,0:T(8,128)(2,1)S(1)}, bf16[1024,768]{1,0:T(8,128)(2,1)}, u32[]{:S(2)}) copy-start(bf16[1024,768]{1,0:T(8,128)(2,1)} %reduce-scatter.9.cloned.1.call-done) | copy-start | bytes 4718596
  1326.3 213.2 %copy-start.33 = (f32[768]{0:T(1024)S(1)}, f32[768]{0:T(1024)}, u32[]{:S(2)}) copy-start(f32[768]{0:T(1024)} %copy-done.32) | copy-start | bytes 9220
  1326.3 213.2 %copy-start.35 = (f32[768]{0:T(1024)S(1)}, f32[768]{0:T(1024)}, u32[]{:S(2)}) copy-start(f32[768]{0:T(1024)} %copy-done.34) | copy-start | bytes 9220
  1471.6 305.4 %collective-permute-start.2 = (f32[13830,128]{1,0:T(8,128)}, f32[13830,128]{1,0:T(8,128)}, u32[]{:S(2)}, u32[]{:S(2)}) collective-permute-start(f32[13830,128]{1,0:T(8,128)} %fusion.144), channel_id=1, source_target_pairs={{0,16},{4,20},{8,24},{12,28},{16,0},{20,4},{24,8},{28,12},{1,17},{... | collective-permute-start | bytes 21242888 | tf_op jit(solution)/shard_map/ppermute | solution.py:332
  1539.5 6.8 dynamic-slice-start
  1542.8 3.5 copy-start.15
  1785.5 7.9 copy-start.16
  (12 other events, 23.9 us)
Sparse Core Ops, SparseCore 0:
  10.9 154.8 all-gather.9
  167.4 44.5 all-gather.5
  213.6 46.4 all-gather.7
  838.3 58.8 reduce-scatter.8
  909.0 58.8 reduce-scatter.10
  974.3 20.7 reduce-scatter.12
  1326.4 57.9 reduce-scatter.6
